TPU v7x, 32 devices: a whole 2x2x4 slice. The times are simulated.
32 devices in a mesh: dp: 16 (over z, y, x), tensor: 2 (over core).
Axes of the slice: x: 2, y: 2, z: 4, core: 2. Of those that a mesh axis runs over, the one named last changes fastest.
Arguments:
- normed: bfloat16 [3072, 8192], P('dp', 'tensor'), may hold values from -6 to 6
- stored_queries: bfloat16 [3072, 4096], P('dp', 'tensor'), may hold values from -170 to 170
- stored_keys: bfloat16 [3072, 1024], P('dp', 'tensor'), may hold values from -7 to 7
- stored_values: bfloat16 [3072, 1024], P('dp', 'tensor'), may hold values from -6 to 6
- head_output_grad: bfloat16 [3072, 4096], P('dp', 'tensor'), may hold values from -6 to 6
- document_index: int32 [16, 192], P('dp'), may hold values from 0 to 7, never falling along the last dimension, each value on 1 to 72 neighbouring positions
- query_projection_weight: bfloat16 [8192, 4096], P('dp', 'tensor'), may hold values from -0.0625 to 0.0625
- key_projection_weight: bfloat16 [8192, 1024], P('dp', 'tensor'), may hold values from -0.0625 to 0.0625
- value_projection_weight: bfloat16 [8192, 1024], P('dp', 'tensor'), may hold values from -0.0625 to 0.0625
- adapter_down_maps: bfloat16 [8192, 192], P('tensor'), may hold values from -0.0625 to 0.0625
- query_up_map: bfloat16 [64, 4096], P(None, 'tensor'), may hold values from -0.75 to 0.75
- key_value_up_maps: bfloat16 [2, 64, 1024], P(None, None, 'tensor'), may hold values from -0.75 to 0.75
Outputs:
- normed_input_grad: bfloat16 [3072, 8192], P('dp', 'tensor')
- down_grad: float32 [8192, 192], P('tensor')
- query_up_grad: float32 [64, 4096], P(None, 'tensor')
- key_value_up_grad: float32 [2, 64, 1024], P(None, None, 'tensor')
All inputs are finite; a program needn't handle non-finite values.
Results may differ from a plain program's by a relative error of at most 0.0095.
Values may be sent and summed in bfloat16 or wider, within the bound.
No kernel may reach another device: no remote copies, remote signals or barrier semaphores. Data moves between devices by JAX's collectives and lax.ppermute only.
A program may use at most 192 MiB of HBM per device.

v0:
```python
import math
import jax
import jax.numpy as jnp
from jax import lax
from jax.sharding import PartitionSpec as P

QUERY_HEADS = 32
KEY_HEADS = 8
HEAD_SIZE = 128
ADAPTER_RANK = 64
adapter_scale = 0.5


def attention_backward(queries, keyrows, value_row_block, output_gradient, ids):
    token_count = queries.shape[0]
    key_value_heads = keyrows.shape[1] // HEAD_SIZE
    query_group = QUERY_HEADS // KEY_HEADS
    scale = 1.0 / math.sqrt(HEAD_SIZE)
    qmat = queries.reshape(token_count, key_value_heads, query_group, HEAD_SIZE)
    kmat = keyrows.reshape(token_count, key_value_heads, HEAD_SIZE)
    value_matrix = value_row_block.reshape(token_count, key_value_heads, HEAD_SIZE)
    output_matrix = output_gradient.reshape(token_count, key_value_heads, query_group, HEAD_SIZE)
    same = ids[:, None] == ids[None, :]
    scores = jnp.einsum("bmav,wmv->mabw", qmat, kmat, preferred_element_type=jnp.float32) * scale
    scores = jnp.where(same[None, None], scores, -1e30)
    probs = jax.nn.softmax(scores, axis=-1)
    probs_half = probs.astype(jnp.bfloat16)
    value_gradient = jnp.einsum(
        "kgtu,tkgd->ukd", probs_half, output_matrix, preferred_element_type=jnp.float32
    ).astype(jnp.bfloat16)
    probability_grad = jnp.einsum(
        "bmav,wmv->mabw", output_matrix, value_matrix, preferred_element_type=jnp.float32
    )
    row_dots = jnp.sum(probs * probability_grad, axis=-1, keepdims=True)
    score_grad = (probs * (probability_grad - row_dots) * scale).astype(jnp.bfloat16)
    query_gradient = jnp.einsum(
        "kgtu,ukd->tkgd", score_grad, kmat, preferred_element_type=jnp.float32
    ).astype(jnp.bfloat16)
    key_gradient = jnp.einsum(
        "kgtu,tkgd->ukd", score_grad, qmat, preferred_element_type=jnp.float32
    ).astype(jnp.bfloat16)
    return (
        query_gradient.reshape(token_count, -1),
        key_gradient.reshape(token_count, -1),
        value_gradient.reshape(token_count, -1),
    )


def rows_product(left, piece):
    return lax.dot_general(
        left, piece, (((1,), (1,)), ((), ())), preferred_element_type=jnp.float32
    )


def adapter_total(
    normed, adapter_middle, middle_gradient, query_gradient, key_gradient, value_gradient
):
    down_local = lax.dot_general(
        normed, middle_gradient, (((0,), (0,)), ((), ())), preferred_element_type=jnp.float32
    )
    local_query = adapter_scale * lax.dot_general(
        adapter_middle[:, 0:ADAPTER_RANK],
        query_gradient,
        (((0,), (0,)), ((), ())),
        preferred_element_type=jnp.float32,
    )
    local_key = adapter_scale * lax.dot_general(
        adapter_middle[:, ADAPTER_RANK : 2 * ADAPTER_RANK],
        key_gradient,
        (((0,), (0,)), ((), ())),
        preferred_element_type=jnp.float32,
    )
    local_value = adapter_scale * lax.dot_general(
        adapter_middle[:, 2 * ADAPTER_RANK : 3 * ADAPTER_RANK],
        value_gradient,
        (((0,), (0,)), ((), ())),
        preferred_element_type=jnp.float32,
    )
    down_total, query_total, key_value_total = lax.psum(
        (down_local, local_query, jnp.stack([local_key, local_value])), "dp"
    )
    return (down_total, query_total, key_value_total)


def shards(
    normed,
    stored_queries,
    stored_keys,
    stored_values,
    head_output_grad,
    document_index,
    query_projection_weight,
    key_projection_weight,
    value_projection_weight,
    adapter_down_maps,
    query_up_map,
    key_value_up_maps,
):
    query_gradient, key_gradient, value_gradient = attention_backward(
        stored_queries, stored_keys, stored_values, head_output_grad, document_index[0]
    )
    local_middle = jnp.dot(normed, adapter_down_maps, preferred_element_type=jnp.float32)
    grad_local = jnp.concatenate(
        [
            adapter_scale * rows_product(query_gradient, query_up_map),
            adapter_scale * rows_product(key_gradient, key_value_up_maps[0]),
            adapter_scale * rows_product(value_gradient, key_value_up_maps[1]),
        ],
        axis=1,
    )
    middle_total, grad_sum = (
        lax.psum(local_middle.astype(jnp.bfloat16), "tensor").astype(jnp.float32),
        lax.psum(grad_local.astype(jnp.bfloat16), "tensor").astype(jnp.float32),
    )
    adapter_middle = middle_total.astype(jnp.bfloat16)
    middle_gradient = grad_sum.astype(jnp.bfloat16)
    base_term = rows_product(
        query_gradient, lax.all_gather(query_projection_weight, "dp", axis=0, tiled=True)
    )
    base_term = base_term + rows_product(
        key_gradient, lax.all_gather(key_projection_weight, "dp", axis=0, tiled=True)
    )
    base_term = base_term + rows_product(
        value_gradient, lax.all_gather(value_projection_weight, "dp", axis=0, tiled=True)
    )
    base_offset = lax.psum_scatter(
        base_term.astype(jnp.bfloat16), "tensor", scatter_dimension=1, tiled=True
    ).astype(jnp.float32)
    normed_input_grad = (
        base_offset
        + lax.dot_general(
            middle_gradient,
            adapter_down_maps,
            (((1,), (1,)), ((), ())),
            preferred_element_type=jnp.float32,
        )
    ).astype(jnp.bfloat16)
    down_total, query_total, key_value_total = adapter_total(
        normed, adapter_middle, middle_gradient, query_gradient, key_gradient, value_gradient
    )
    return (normed_input_grad, down_total, query_total, key_value_total)


def solution(mesh):
    in_specs = (
        P("dp", "tensor"),
        P("dp", "tensor"),
        P("dp", "tensor"),
        P("dp", "tensor"),
        P("dp", "tensor"),
        P("dp", None),
        P("dp", "tensor"),
        P("dp", "tensor"),
        P("dp", "tensor"),
        P("tensor", None),
        P(None, "tensor"),
        P(None, None, "tensor"),
    )
    out_specs = (P("dp", "tensor"), P("tensor", None), P(None, "tensor"), P(None, None, "tensor"))
    return jax.shard_map(shards, mesh=mesh, in_specs=in_specs, out_specs=out_specs, check_vma=False)
```

profile of v0, /device:TPU:0, one launch (start us, length us, event | category | flops | bytes accessed | tf_op | source)
XLA Modules:
  0.0 785.0 jit_solution(11246477289122399510)
XLA Ops:
  8.0 0.0 all-gather.4.cloned.1.call-start
  8.1 0.7 all-gather.4.cloned.1.call-update
  8.8 0.0 all-gather.6.cloned.1.call-start
  8.8 0.7 all-gather.6.cloned.1.call-update
  9.5 0.0 all-gather.8.cloned.1.call-start
  9.6 0.7 all-gather.8.cloned.1.call-update
  10.3 0.0 all-reduce.7.cloned.1.call-start
  10.3 0.6 reshape.65
  10.9 2.6 reshape.63
  13.5 0.1 reshape.62
  13.6 1.2 reshape.64
  14.8 0.1 broadcast_compare_fusion
  14.9 0.6 fusion.37
  15.5 2.2 fusion.34
  17.7 2.6 fusion.67
  20.3 7.6 fusion.15
  27.9 0.6 copy.30
  28.5 0.6 reshape.66
  29.2 6.3 fusion.24
  35.5 2.7 fusion.25
  38.2 0.2 fusion.32
  38.4 0.2 fusion.31
  38.6 0.4 fusion.30
  38.9 0.7 pad_maximum_fusion.1
  39.6 1.2 convolution_convert_fusion.1
  40.8 0.0 all-reduce.7.cloned.1.call-update
  40.9 0.2 reduce-scatter.2.cloned.1.call-start
  41.1 324.1 %all-gather.4.cloned.1.call-done = bf16[8192,2048]{1,0:T(8,128)(2,1)} async-done(((bf16[512,2048]{1,0:T(8,128)(2,1)}), bf16[8192,2048]{1,0:T(8,128)(2,1)}) %all-gather.4.cloned.1.call-update) | async-done | bytes 33554448 | tf_op jit(solution)/shard_map/all_gather | solution.py:118
  365.2 18.4 %fusion.68 = f32[192,8192]{1,0:T(8,128)} fusion(bf16[192,2048]{1,0:T(8,128)(2,1)S(1)} %reshape.66, bf16[8192,2048]{1,0:T(8,128)(2,1)} %all-gather.4.cloned.1.call-done), kind=kOutput, calls=%fused_computation.82 | convolution fusion | flops 6442450944 | bytes 40632320 | tf_op jit(solution)/shard_map/dot_general | solution.py:50
  383.6 95.4 %all-gather.6.cloned.1.call-done = bf16[8192,512]{1,0:T(8,128)(2,1)} async-done(((bf16[512,512]{1,0:T(8,128)(2,1)}), bf16[8192,512]{1,0:T(8,128)(2,1)}) %all-gather.6.cloned.1.call-update) | async-done | bytes 8388624 | tf_op jit(solution)/shard_map/all_gather | solution.py:121
  479.1 10.6 %convolution_add_fusion.1 = f32[192,8192]{1,0:T(8,128)} fusion(f32[192,8192]{1,0:T(8,128)} %fusion.68, bf16[8192,512]{1,0:T(8,128)(2,1)} %all-gather.6.cloned.1.call-done, bf16[4,24,8,128]{3,2,1,0:T(8,128)(2,1)S(1)} %fusion.24), kind=kOutput, calls=%fused_computation.3 | convolution fusion | flops 1612185600 | bytes 21168128 | tf_op jit(solution)/shard_map/dot_general | solution.py:50
  489.7 103.2 %all-gather.8.cloned.1.call-done = bf16[8192,512]{1,0:T(8,128)(2,1)} async-done(((bf16[512,512]{1,0:T(8,128)(2,1)}), bf16[8192,512]{1,0:T(8,128)(2,1)}) %all-gather.8.cloned.1.call-update) | async-done | bytes 8388624 | tf_op jit(solution)/shard_map/all_gather | solution.py:124
  592.9 9.7 %fusion.2 = bf16[192,8192]{1,0:T(8,128)(2,1)} fusion(f32[192,8192]{1,0:T(8,128)} %convolution_add_fusion.1, bf16[8192,512]{1,0:T(8,128)(2,1)} %all-gather.8.cloned.1.call-done, bf16[4,24,8,128]{3,2,1,0:T(8,128)(2,1)S(1)} %fusion.25), kind=kOutput, calls=%fused_computation.4 | convolution fusion | flops 1613758464 | bytes 18022400 | tf_op jit(solution)/shard_map/dot_general | solution.py:50
  602.6 0.0 reduce-scatter.2.cloned.1.call-update
  602.6 0.0 all-reduce.5.cloned.1.call-start
  602.7 0.0 all-reduce.7.cloned.1.call-done
  602.7 1.0 fusion.28
  603.7 1.1 fusion.29
  604.8 0.7 pad_maximum_fusion
  605.5 1.9 convolution_multiply_fusion
  607.4 3.1 convolution_bitcast_fusion
  610.5 1.1 reduce-scatter.2.cloned.1.call-done
  611.7 0.4 copy-done.5
  612.0 3.2 fusion.3
  615.2 157.2 %all-reduce.5.cloned.1.call-done = (f32[4096,192]{0,1:T(8,128)}, f32[64,2048]{1,0:T(8,128)}, f32[2,64,512]{2,1,0:T(8,128)}) async-done(((f32[4096,192]{0,1:T(8,128)}, f32[64,2048]{1,0:T(8,128)}, f32[2,64,512]{2,1,0:T(8,128)}), (f32[4096,192]{0,1:T(8,128)}, f32[64,2048]{1,0:T(8,128)}, f32[2,64,512]{2,1,0:T(8,128)})) %all-reduce.5.cloned.1.call-update) | async-done | bytes 3932176 | tf_op jit(solution)/shard_map/psum | solution.py:79
  772.4 3.9 copy.92
  776.4 0.8 copy.93
  777.2 0.7 copy.94
  (28 shorter events, 0.1 us)
Async XLA Ops:
  8.0 31.6 %copy-start = (bf16[192,4096]{1,0:T(8,128)(2,1)S(1)}, bf16[192,4096]{1,0:T(8,128)(2,1)}, u32[]{:S(2)}) copy-start(bf16[192,4096]{1,0:T(8,128)(2,1)} %param.12) | copy-start | bytes 4718596
  8.0 2.3 copy-start.6
  8.0 5.5 copy-start.11
  8.0 6.7 copy-start.12
  8.0 357.2 %all-gather.4.cloned.1.call-start = ((), (), s32[]{:S(2)}) async-start(), calls=%async_computation.1 | async-start | bytes 35651584 | tf_op jit(solution)/shard_map/all_gather | solution.py:118
  8.8 470.3 %all-gather.6.cloned.1.call-start = ((), (), s32[]{:S(2)}) async-start(), calls=%async_computation.2 | async-start | bytes 8912896 | tf_op jit(solution)/shard_map/all_gather | solution.py:121
  9.5 583.4 %all-gather.8.cloned.1.call-start = ((), (), s32[]{:S(2)}) async-start(), calls=%async_computation.3 | async-start | bytes 8912896 | tf_op jit(solution)/shard_map/all_gather | solution.py:124
  10.3 592.4 %all-reduce.7.cloned.1.call-start = ((), (), s32[]{:S(2)}) async-start(), calls=%async_computation.6 | async-start | bytes 393216 | tf_op jit(solution)/shard_map/psum | solution.py:113
  10.9 4.6 copy-start.1
  13.5 4.2 copy-start.3
  29.1 6.3 copy-start.2
  35.4 2.7 copy-start.13
  35.5 3.1 copy-start.10
  35.5 4.1 copy-start.4
  40.9 570.8 %reduce-scatter.2.cloned.1.call-start = ((), (), s32[]{:S(2)}) async-start(), calls=%async_computation.4 | async-start | bytes 4718592 | tf_op jit(solution)/shard_map/reduce_scatter | solution.py:126
  602.6 169.8 %all-reduce.5.cloned.1.call-start = ((), (), s32[]{:S(2)}) async-start(), calls=%async_computation.5 | async-start | bytes 7864320 | tf_op jit(solution)/shard_map/psum | solution.py:79
  610.5 1.5 copy-start.5
  610.5 1.5 copy-start.8
  772.4 3.9 copy-start.7
  772.4 4.7 copy-start.9
Sparse Core Ops, SparseCore 0:
  11.7 353.5 all-gather.3
  368.0 111.0 all-gather.5
  481.8 111.0 all-gather.7
  610.9 161.4 all-reduce.4
Sparse Core Ops, SparseCore 1:
  41.0 20.6 all-reduce.6
  602.7 8.9 reduce-scatter.1
where the time goes:
time: 785 us
  waiting for transfers between devices  683 us (87%)
  matrix products  70.3 us (9%)
  between operations  15.4 us (2%)
  local copies, waits for them, and re-layouts  11.5 us (1%)
    all_gather x1, waiting for transfers between devices, shards(): lax.all_gather(query_projection_weight, 'dp', axis=0, tiled=True)  324 us
    psum x1, waiting for transfers between devices, adapter_total(): lax.psum((down_local, local_query, jnp.stack([local_key, local_value])),...  157 us
    all_gather x1, waiting for transfers between devices, shards(): lax.all_gather(value_projection_weight, 'dp', axis=0, tiled=True)  103 us
    all_gather x1, waiting for transfers between devices, shards(): lax.all_gather(key_projection_weight, 'dp', axis=0, tiled=True)  95.4 us
    dot_general x6, matrix products, rows_product(): lax.dot_general(left, piece, (((1,), (1,)), ((), ())), preferred_element_...  39.5 us
  transfers between devices with their start and end apart: 6, of which 5 were waited for; matrix products, arithmetic and copies ran while one was open for 10% of the time, Pallas kernels for 0%

commit v1 on v0

--- a/solution.py
+++ b/solution.py
@@ -1,3 +1,4 @@
+import functools
 import math
 import jax
 import jax.numpy as jnp
@@ -9,6 +10,25 @@
 HEAD_SIZE = 128
 ADAPTER_RANK = 64
 adapter_scale = 0.5
+
+
+def wait_units_over_axis(mine, dim_i):
+    n_shards = lax.axis_size("dp")
+    xs_all = list(map(lambda no: (no, (no + 1) % n_shards), range(n_shards)))
+    buffer = list(map(lambda no: (no, (no - 1) % n_shards), range(n_shards)))
+    wide_out, r2 = ([mine], [mine])
+    for _ in range(n_shards // 2):
+        wide_out.append(lax.ppermute(wide_out[-1], axis_name="dp", perm=xs_all))
+    for _ in range((n_shards - 1) // 2):
+        r2.append(lax.ppermute(r2[-1], axis_name="dp", perm=buffer))
+    newest = jnp.concatenate([*wide_out[::-1], *r2[1:]], axis=dim_i)
+    odd = jnp.roll(
+        newest, shift=(lax.axis_index("dp") - n_shards // 2) * mine.shape[dim_i], axis=dim_i
+    )
+    return odd
+
+
+_search_node = functools.partial(wait_units_over_axis, dim_i=0)
 
 
 def attention_backward(queries, keyrows, value_row_block, output_gradient, ids):
@@ -114,9 +134,7 @@
     )
     adapter_middle = middle_total.astype(jnp.bfloat16)
     middle_gradient = grad_sum.astype(jnp.bfloat16)
-    base_term = rows_product(
-        query_gradient, lax.all_gather(query_projection_weight, "dp", axis=0, tiled=True)
-    )
+    base_term = rows_product(query_gradient, _search_node(query_projection_weight))
     base_term = base_term + rows_product(
         key_gradient, lax.all_gather(key_projection_weight, "dp", axis=0, tiled=True)
     )

time: 785 us -> 1100 us (1.40)
  waiting for transfers between devices: 683 us -> 850 us
  local copies, waits for them, and re-layouts: 11.5 us -> 98.8 us
  starting transfers between devices: 0.42 us -> 59 us
    ppermute x0 -> x15, waiting for transfers between devices: none -> 684 us  [the longest x8 684 us: wait_units_over_axis(): wide_out.append(lax.ppermute(wide_out[-1], axis_name='dp', perm=xs_all))]
    all_gather x1 -> x0, waiting for transfers between devices: 324 us -> none  [shards(): lax.all_gather(query_projection_weight, 'dp', axis=0, tiled=True)]
    all_gather x1, waiting for transfers between devices: 103 us -> 0.01 us  [shards(): lax.all_gather(value_projection_weight, 'dp', axis=0, tiled=True)]
    all_gather x1, waiting for transfers between devices: 95.4 us -> 0.01 us  [shards(): lax.all_gather(key_projection_weight, 'dp', axis=0, tiled=True)]
    unnamed x31 -> x90, local copies, waits for them, and re-layouts: 5.85 us -> 87.5 us
    ppermute x0 -> x15, starting transfers between devices: none -> 58.7 us  [the longest x7 40.8 us: wait_units_over_axis(): r2.append(lax.ppermute(r2[-1], axis_name='dp', perm=buffer))]
  transfers between devices with their start and end apart: 6 -> 20, of which waited for: 5 -> 10; matrix products, arithmetic and copies ran while one was open for 10% -> 15% of each run, Pallas kernels for 0% -> 0%
where the time goes in v1:
time: 1100 us
  waiting for transfers between devices  850 us (77%)
  local copies, waits for them, and re-layouts  98.8 us (9%)
  matrix products  68.8 us (6%)
  starting transfers between devices  59 us (5%)
  between operations  15.5 us (1%)
    ppermute x8, waiting for transfers between devices, wait_units_over_axis(): wide_out.append(lax.ppermute(wide_out[-1], axis_name='dp', perm=xs_all))  684 us
    psum x1, waiting for transfers between devices, adapter_total(): lax.psum((down_local, local_query, jnp.stack([local_key, local_value])),...  157 us
    unnamed x90, local copies, waits for them, and re-layouts  87.5 us
    ppermute x7, starting transfers between devices, wait_units_over_axis(): r2.append(lax.ppermute(r2[-1], axis_name='dp', perm=buffer))  40.8 us
    dot_general x6, matrix products, rows_product(): lax.dot_general(left, piece, (((1,), (1,)), ((), ())), preferred_element_...  40.4 us
  transfers between devices with their start and end apart: 20, of which 10 were waited for; matrix products, arithmetic and copies ran while one was open for 15% of the time, Pallas kernels for 0%

profile of v1, /device:TPU:0, one launch (start us, length us, event | category | flops | bytes accessed | tf_op | source)
XLA Modules:
  0.0 1099.8 jit_solution(2152764267661387155)
XLA Ops:
  9.5 3.0 collective-permute-start
  12.5 75.2 %collective-permute-done = bf16[512,2048]{1,0:T(8,128)(2,1)S(1)} collective-permute-done((bf16[512,2048]{1,0:T(8,128)(2,1)}, bf16[512,2048]{1,0:T(8,128)(2,1)S(1)}, u32[]{:S(2)}, u32[]{:S(2)}) %collective-permute-start) | collective-permute-done | bytes 2097184 | tf_op jit(solution)/shard_map/ppermute | solution.py:21
  89.1 5.6 collective-permute-start.8
  94.7 112.6 %collective-permute-done.1 = bf16[512,2048]{1,0:T(8,128)(2,1)S(1)} collective-permute-done((bf16[512,2048]{1,0:T(8,128)(2,1)S(1)}, bf16[512,2048]{1,0:T(8,128)(2,1)S(1)}, u32[]{:S(2)}, u32[]{:S(2)}) %collective-permute-start.1) | collective-permute-done | bytes 2097184 | tf_op jit(solution)/shard_map/ppermute | solution.py:21
  207.3 2.5 collective-permute-start.2
  211.1 5.4 collective-permute-start.9
  216.4 99.1 %collective-permute-done.2 = bf16[512,2048]{1,0:T(8,128)(2,1)S(1)} collective-permute-done((bf16[512,2048]{1,0:T(8,128)(2,1)S(1)}, bf16[512,2048]{1,0:T(8,128)(2,1)S(1)}, u32[]{:S(2)}, u32[]{:S(2)}) %collective-permute-start.2) | collective-permute-done | bytes 2097184 | tf_op jit(solution)/shard_map/ppermute | solution.py:21
  315.6 2.5 collective-permute-start.3
  318.1 7.9 collective-permute-start.10
  326.0 111.5 %collective-permute-done.3 = bf16[512,2048]{1,0:T(8,128)(2,1)S(1)} collective-permute-done((bf16[512,2048]{1,0:T(8,128)(2,1)S(1)}, bf16[512,2048]{1,0:T(8,128)(2,1)S(1)}, u32[]{:S(2)}, u32[]{:S(2)}) %collective-permute-start.3) | collective-permute-done | bytes 2097184 | tf_op jit(solution)/shard_map/ppermute | solution.py:21
  440.0 7.0 collective-permute-start.11
  447.0 82.1 %collective-permute-done.4 = bf16[512,2048]{1,0:T(8,128)(2,1)} collective-permute-done((bf16[512,2048]{1,0:T(8,128)(2,1)S(1)}, bf16[512,2048]{1,0:T(8,128)(2,1)}, u32[]{:S(2)}, u32[]{:S(2)}) %collective-permute-start.4) | collective-permute-done | bytes 2097184 | tf_op jit(solution)/shard_map/ppermute | solution.py:21
  529.1 2.6 collective-permute-start.5
  531.7 5.7 collective-permute-start.12
  545.0 74.5 %collective-permute-done.5 = bf16[512,2048]{1,0:T(8,128)(2,1)} collective-permute-done((bf16[512,2048]{1,0:T(8,128)(2,1)}, bf16[512,2048]{1,0:T(8,128)(2,1)}, u32[]{:S(2)}, u32[]{:S(2)}) %collective-permute-start.5) | collective-permute-done | bytes 2097184 | tf_op jit(solution)/shard_map/ppermute | solution.py:21
  624.3 2.6 fusion.79
  627.0 3.1 collective-permute-start.13
  630.1 6.0 fusion.24
  637.3 6.2 fusion.33
  643.8 2.7 fusion.34
  646.5 65.8 %collective-permute-done.6 = bf16[512,2048]{1,0:T(8,128)(2,1)} collective-permute-done((bf16[512,2048]{1,0:T(8,128)(2,1)}, bf16[512,2048]{1,0:T(8,128)(2,1)}, u32[]{:S(2)}, u32[]{:S(2)}) %collective-permute-start.6) | collective-permute-done | bytes 2097184 | tf_op jit(solution)/shard_map/ppermute | solution.py:21
  712.3 2.5 collective-permute-start.7
  717.4 6.0 collective-permute-start.14
  723.4 8.9 fusion.54
  732.3 8.9 fusion.50
  741.2 63.0 %collective-permute-done.7 = bf16[512,2048]{1,0:T(8,128)(2,1)} collective-permute-done((bf16[512,2048]{1,0:T(8,128)(2,1)}, bf16[512,2048]{1,0:T(8,128)(2,1)}, u32[]{:S(2)}, u32[]{:S(2)}) %collective-permute-start.7) | collective-permute-done | bytes 2097184 | tf_op jit(solution)/shard_map/ppermute | solution.py:21
  804.3 3.2 constant_dynamic-update-slice_fusion.31
  807.5 3.2 constant_dynamic-update-slice_fusion.30
  810.6 3.2 constant_dynamic-update-slice_fusion.29
  813.9 3.4 constant_dynamic-update-slice_fusion.28
  835.2 3.2 constant_dynamic-update-slice_fusion.19
  838.4 3.2 constant_dynamic-update-slice_fusion.18
  841.7 3.1 constant_dynamic-update-slice_fusion.17
  844.8 3.2 constant_dynamic-update-slice_fusion.16
  848.0 3.2 constant_dynamic-update-slice_fusion.15
  851.2 3.2 constant_dynamic-update-slice_fusion.14
  854.3 3.1 constant_dynamic-update-slice_fusion.13
  857.5 3.2 constant_dynamic-update-slice_fusion.12
  872.6 3.2 constant_dynamic-update-slice_fusion.3
  875.8 3.2 constant_dynamic-update-slice_fusion.2
  879.0 3.2 constant_dynamic-update-slice_fusion.1
  882.2 3.2 constant_dynamic-update-slice_fusion
  885.4 21.9 %fusion.10 = bf16[192,8192]{1,0:T(8,128)(2,1)} fusion(f32[192,8192]{1,0:T(8,128)} %fusion.50, f32[192,8192]{1,0:T(8,128)} %fusion.54, bf16[192,2048]{1,0:T(8,128)(2,1)S(1)} %reshape.66, bf16[16384,2048]{1,0:T(8,128)(2,1)} %constant_dynamic-update-slice_fusion, s32[]{:T(128)S(6)} %select_n.19), kind=kOutput, calls=%fused_computation.6 | convolution fusion | flops 6447169536 | bytes 50069508 | tf_op jit(solution)/shard_map/dot_general | solution.py:70
  912.0 3.1 convolution_bitcast_fusion
  918.9 7.3 reduce-scatter.2.cloned.1.call-done
  926.2 3.9 add_convert_fusion
  930.0 157.2 %all-reduce.5.cloned.1.call-done = (f32[4096,192]{0,1:T(8,128)}, f32[64,2048]{1,0:T(8,128)}, f32[2,64,512]{2,1,0:T(8,128)}) async-done(((f32[4096,192]{0,1:T(8,128)}, f32[64,2048]{1,0:T(8,128)}, f32[2,64,512]{2,1,0:T(8,128)}), (f32[4096,192]{0,1:T(8,128)}, f32[64,2048]{1,0:T(8,128)}, f32[2,64,512]{2,1,0:T(8,128)})) %all-reduce.5.cloned.1.call-update) | async-done | bytes 3932176 | tf_op jit(solution)/shard_map/psum | solution.py:99
  1087.3 3.9 copy.123
  (116 shorter events, 62.8 us)
Async XLA Ops:
  8.0 708.0 %copy-start = (bf16[192,4096]{1,0:T(8,128)(2,1)S(1)}, bf16[192,4096]{1,0:T(8,128)(2,1)}, u32[]{:S(2)}) copy-start(bf16[192,4096]{1,0:T(8,128)(2,1)} %param.12) | copy-start | bytes 4718596
  8.0 715.4 %all-gather.3.cloned.1.call-start = ((), (), s32[]{:S(2)}) async-start(), calls=%async_computation.1 | async-start | bytes 8912896 | tf_op jit(solution)/shard_map/all_gather | solution.py:139
  8.7 723.6 %all-gather.5.cloned.1.call-start = ((), (), s32[]{:S(2)}) async-start(), calls=%async_computation.2 | async-start | bytes 8912896 | tf_op jit(solution)/shard_map/all_gather | solution.py:142
  9.5 897.9 %all-reduce.7.cloned.1.call-start = ((), (), s32[]{:S(2)}) async-start(), calls=%async_computation.5 | async-start | bytes 393216 | tf_op jit(solution)/shard_map/psum | solution.py:133
  9.5 78.2 %collective-permute-start = (bf16[512,2048]{1,0:T(8,128)(2,1)}, bf16[512,2048]{1,0:T(8,128)(2,1)S(1)}, u32[]{:S(2)}, u32[]{:S(2)}) collective-permute-start(bf16[512,2048]{1,0:T(8,128)(2,1)} %param.18), channel_id=1, source_target_pairs={{0,2},{2,4},{4,6},{6,8},{8,10},{10,12},{12,14},{14,16},{16,18},{18... | collective-permute-start | bytes 6291464 | tf_op jit(solution)/shard_map/ppermute | solution.py:21
  87.8 1.3 copy-start.2
  89.1 118.2 %collective-permute-start.1 = (bf16[512,2048]{1,0:T(8,128)(2,1)S(1)}, bf16[512,2048]{1,0:T(8,128)(2,1)S(1)}, u32[]{:S(2)}, u32[]{:S(2)}) collective-permute-start(bf16[512,2048]{1,0:T(8,128)(2,1)S(1)} %collective-permute-done), channel_id=1, source_target_pairs={{0,2},{2,4},{4,6},{6,8},{8,10},{10,12},{12,14},{14,16},{16,18},{18... | collective-permute-start | bytes 6291464 | tf_op jit(solution)/shard_map/ppermute | solution.py:21
  89.1 120.7 %collective-permute-start.8 = (bf16[512,2048]{1,0:T(8,128)(2,1)}, bf16[512,2048]{1,0:T(8,128)(2,1)S(1)}, u32[]{:S(2)}, u32[]{:S(2)}) collective-permute-start(bf16[512,2048]{1,0:T(8,128)(2,1)} %param.18), channel_id=1, source_target_pairs={{0,30},{2,0},{4,2},{6,4},{8,6},{10,8},{12,10},{14,12},{16,14},{18,... | collective-permute-start | bytes 6291464 | tf_op jit(solution)/shard_map/ppermute | solution.py:23
  207.3 110.8 %copy-start.6 = (bf16[512,2048]{1,0:T(8,128)(2,1)}, bf16[512,2048]{1,0:T(8,128)(2,1)S(1)}, u32[]{:S(2)}) copy-start(bf16[512,2048]{1,0:T(8,128)(2,1)S(1)} %collective-permute-done.1) | copy-start | bytes 6291460
  207.3 108.3 %collective-permute-start.2 = (bf16[512,2048]{1,0:T(8,128)(2,1)S(1)}, bf16[512,2048]{1,0:T(8,128)(2,1)S(1)}, u32[]{:S(2)}, u32[]{:S(2)}) collective-permute-start(bf16[512,2048]{1,0:T(8,128)(2,1)S(1)} %collective-permute-done.1), channel_id=1, source_target_pairs={{0,2},{2,4},{4,6},{6,8},{8,10},{10,12},{12,14},{14,16},{16,18},{18... | collective-permute-start | bytes 6291464 | tf_op jit(solution)/shard_map/ppermute | solution.py:21
  209.8 1.3 copy-start.4
  211.1 107.0 %collective-permute-start.9 = (bf16[512,2048]{1,0:T(8,128)(2,1)S(1)}, bf16[512,2048]{1,0:T(8,128)(2,1)S(1)}, u32[]{:S(2)}, u32[]{:S(2)}) collective-permute-start(bf16[512,2048]{1,0:T(8,128)(2,1)S(1)} %collective-permute-done.8), channel_id=1, source_target_pairs={{0,30},{2,0},{4,2},{6,4},{8,6},{10,8},{12,10},{14,12},{16,14},{18,... | collective-permute-start | bytes 6291464 | tf_op jit(solution)/shard_map/ppermute | solution.py:23
  315.6 124.4 %copy-start.10 = (bf16[512,2048]{1,0:T(8,128)(2,1)}, bf16[512,2048]{1,0:T(8,128)(2,1)S(1)}, u32[]{:S(2)}) copy-start(bf16[512,2048]{1,0:T(8,128)(2,1)S(1)} %collective-permute-done.2) | copy-start | bytes 6291460
  315.6 121.9 %collective-permute-start.3 = (bf16[512,2048]{1,0:T(8,128)(2,1)S(1)}, bf16[512,2048]{1,0:T(8,128)(2,1)S(1)}, u32[]{:S(2)}, u32[]{:S(2)}) collective-permute-start(bf16[512,2048]{1,0:T(8,128)(2,1)S(1)} %collective-permute-done.2), channel_id=1, source_target_pairs={{0,2},{2,4},{4,6},{6,8},{8,10},{10,12},{12,14},{14,16},{16,18},{18... | collective-permute-start | bytes 6291464 | tf_op jit(solution)/shard_map/ppermute | solution.py:21
  318.1 7.9 copy-start.8
  318.1 121.9 %collective-permute-start.10 = (bf16[512,2048]{1,0:T(8,128)(2,1)S(1)}, bf16[512,2048]{1,0:T(8,128)(2,1)S(1)}, u32[]{:S(2)}, u32[]{:S(2)}) collective-permute-start(bf16[512,2048]{1,0:T(8,128)(2,1)S(1)} %collective-permute-done.9), channel_id=1, source_target_pairs={{0,30},{2,0},{4,2},{6,4},{8,6},{10,8},{12,10},{14,12},{16,14},{18,... | collective-permute-start | bytes 6291464 | tf_op jit(solution)/shard_map/ppermute | solution.py:23
  437.5 94.2 %copy-start.14 = (bf16[512,2048]{1,0:T(8,128)(2,1)}, bf16[512,2048]{1,0:T(8,128)(2,1)S(1)}, u32[]{:S(2)}) copy-start(bf16[512,2048]{1,0:T(8,128)(2,1)S(1)} %collective-permute-done.3) | copy-start | bytes 6291460
  437.5 91.6 %collective-permute-start.4 = (bf16[512,2048]{1,0:T(8,128)(2,1)S(1)}, bf16[512,2048]{1,0:T(8,128)(2,1)}, u32[]{:S(2)}, u32[]{:S(2)}) collective-permute-start(bf16[512,2048]{1,0:T(8,128)(2,1)S(1)} %collective-permute-done.3), channel_id=1, source_target_pairs={{0,2},{2,4},{4,6},{6,8},{8,10},{10,12},{12,14},{14,16},{16,18},{18... | collective-permute-start | bytes 6291464 | tf_op jit(solution)/shard_map/ppermute | solution.py:21
  440.0 7.0 copy-start.12
  440.0 91.7 %collective-permute-start.11 = (bf16[512,2048]{1,0:T(8,128)(2,1)S(1)}, bf16[512,2048]{1,0:T(8,128)(2,1)}, u32[]{:S(2)}, u32[]{:S(2)}) collective-permute-start(bf16[512,2048]{1,0:T(8,128)(2,1)S(1)} %collective-permute-done.10), channel_id=1, source_target_pairs={{0,30},{2,0},{4,2},{6,4},{8,6},{10,8},{12,10},{14,12},{16,14},{18,... | collective-permute-start | bytes 6291464 | tf_op jit(solution)/shard_map/ppermute | solution.py:23
  529.1 90.4 %collective-permute-start.5 = (bf16[512,2048]{1,0:T(8,128)(2,1)}, bf16[512,2048]{1,0:T(8,128)(2,1)}, u32[]{:S(2)}, u32[]{:S(2)}) collective-permute-start(bf16[512,2048]{1,0:T(8,128)(2,1)} %collective-permute-done.4), channel_id=1, source_target_pairs={{0,2},{2,4},{4,6},{6,8},{8,10},{10,12},{12,14},{14,16},{16,18},{18... | collective-permute-start | bytes 6291464 | tf_op jit(solution)/shard_map/ppermute | solution.py:21
  531.7 95.3 %collective-permute-start.12 = (bf16[512,2048]{1,0:T(8,128)(2,1)}, bf16[512,2048]{1,0:T(8,128)(2,1)}, u32[]{:S(2)}, u32[]{:S(2)}) collective-permute-start(bf16[512,2048]{1,0:T(8,128)(2,1)} %collective-permute-done.11), channel_id=1, source_target_pairs={{0,30},{2,0},{4,2},{6,4},{8,6},{10,8},{12,10},{14,12},{16,14},{18,... | collective-permute-start | bytes 6291464 | tf_op jit(solution)/shard_map/ppermute | solution.py:23
  539.7 5.3 copy-start.18
  540.9 81.1 %copy-start.25 = (s32[1,192]{1,0:T(1,128)S(1)}, s32[1,192]{1,0:T(1,128)}, u32[]{:S(2)}) copy-start(s32[1,192]{1,0:T(1,128)} %param.17) | copy-start | bytes 2308
  543.2 81.1 %copy-start.16 = (bf16[192,4,4,128]{3,2,1,0:T(4,128)(2,1)}, bf16[192,4,4,128]{3,2,1,0:T(4,128)(2,1)S(1)}, u32[]{:S(2)}) copy-start(bf16[192,4,4,128]{3,2,1,0:T(4,128)(2,1)S(1)} %reshape.65) | copy-start | bytes 2359300
  619.5 92.8 %collective-permute-start.6 = (bf16[512,2048]{1,0:T(8,128)(2,1)}, bf16[512,2048]{1,0:T(8,128)(2,1)}, u32[]{:S(2)}, u32[]{:S(2)}) collective-permute-start(bf16[512,2048]{1,0:T(8,128)(2,1)} %collective-permute-done.5), channel_id=1, source_target_pairs={{0,2},{2,4},{4,6},{6,8},{8,10},{10,12},{12,14},{14,16},{16,18},{18... | collective-permute-start | bytes 6291464 | tf_op jit(solution)/shard_map/ppermute | solution.py:21
  627.0 90.4 %collective-permute-start.13 = (bf16[512,2048]{1,0:T(8,128)(2,1)}, bf16[512,2048]{1,0:T(8,128)(2,1)}, u32[]{:S(2)}, u32[]{:S(2)}) collective-permute-start(bf16[512,2048]{1,0:T(8,128)(2,1)} %collective-permute-done.12), channel_id=1, source_target_pairs={{0,30},{2,0},{4,2},{6,4},{8,6},{10,8},{12,10},{14,12},{16,14},{18,... | collective-permute-start | bytes 6291464 | tf_op jit(solution)/shard_map/ppermute | solution.py:23
  637.3 6.3 copy-start.26
  637.3 6.5 copy-start.17
  643.8 71.0 %copy-start.27 = (bf16[2,64,512]{2,1,0:T(8,128)(2,1)S(1)}, bf16[2,64,512]{2,1,0:T(8,128)(2,1)}, u32[]{:S(2)}) copy-start(bf16[2,64,512]{2,1,0:T(8,128)(2,1)} %param.23) | copy-start | bytes 393220
  643.8 71.1 %copy-start.24 = (bf16[64,2048]{1,0:T(8,128)(2,1)S(1)}, bf16[64,2048]{1,0:T(8,128)(2,1)}, u32[]{:S(2)}) copy-start(bf16[64,2048]{1,0:T(8,128)(2,1)} %param.22) | copy-start | bytes 786436
  643.8 72.2 %copy-start.19 = (bf16[4096,192]{0,1:T(8,128)(2,1)S(1)}, bf16[4096,192]{0,1:T(8,128)(2,1)}, u32[]{:S(2)}) copy-start(bf16[4096,192]{0,1:T(8,128)(2,1)} %param.21) | copy-start | bytes 4718596
  712.3 92.0 %collective-permute-start.7 = (bf16[512,2048]{1,0:T(8,128)(2,1)}, bf16[512,2048]{1,0:T(8,128)(2,1)}, u32[]{:S(2)}, u32[]{:S(2)}) collective-permute-start(bf16[512,2048]{1,0:T(8,128)(2,1)} %collective-permute-done.6), channel_id=1, source_target_pairs={{0,2},{2,4},{4,6},{6,8},{8,10},{10,12},{12,14},{14,16},{16,18},{18... | collective-permute-start | bytes 6291464 | tf_op jit(solution)/shard_map/ppermute | solution.py:21
  717.3 208.9 %reduce-scatter.2.cloned.1.call-start = ((), (), s32[]{:S(2)}) async-start(), calls=%async_computation.3 | async-start | bytes 4718592 | tf_op jit(solution)/shard_map/reduce_scatter | solution.py:144
  717.4 127.4 %collective-permute-start.14 = (bf16[512,2048]{1,0:T(8,128)(2,1)}, bf16[512,2048]{1,0:T(8,128)(2,1)}, u32[]{:S(2)}, u32[]{:S(2)}) collective-permute-start(bf16[512,2048]{1,0:T(8,128)(2,1)} %collective-permute-done.13), channel_id=1, source_target_pairs={{0,30},{2,0},{4,2},{6,4},{8,6},{10,8},{12,10},{14,12},{16,14},{18,... | collective-permute-start | bytes 6291464 | tf_op jit(solution)/shard_map/ppermute | solution.py:23
  813.8 3.4 copy-start.15
  817.3 2.3 copy-start.11
  819.6 2.3 copy-start.7
  822.0 2.3 copy-start.3
  824.3 2.3 copy-start.1
  826.6 2.3 copy-start.5
  829.0 2.3 copy-start.9
  831.3 2.3 copy-start.13
  907.3 180.0 %all-reduce.5.cloned.1.call-start = ((), (), s32[]{:S(2)}) async-start(), calls=%async_computation.4 | async-start | bytes 7864320 | tf_op jit(solution)/shard_map/psum | solution.py:99
  915.2 1.4 copy-start.20
  915.2 1.4 copy-start.22
  1087.3 3.9 copy-start.21
  1087.3 4.7 copy-start.23
Sparse Core Ops, SparseCore 0:
  11.6 185.5 all-gather.2
  200.0 248.4 all-gather.4
  915.9 171.3 all-reduce.4
Sparse Core Ops, SparseCore 1:
  717.4 71.8 all-reduce.6
  907.4 18.7 reduce-scatter.1
